TPU v7x, 256 devices: a whole 4x4x8 slice. The times are simulated.
256 devices in a mesh: dp: 32 (over y, z), vocab: 8 (over x, core).
Axes of the slice: x: 4, y: 4, z: 8, core: 2. Of those that a mesh axis runs over, the one named last changes fastest.
Arguments:
- draft_logits: bfloat16 [4096, 128000], P('dp', 'vocab'), may hold values from -15 to 250
- hidden: bfloat16 [4096, 2304], P('dp'), may hold values from -40 to 40
- embed_cot: bfloat16 [4096, 2304], P('dp'), may hold values from -0.59765625 to 0.59765625
- draft_ids: int32 [4096], P('dp'), may hold values from 0 to 127999, as said below
- target_ids: int32 [4096, 32], P('dp'), may hold values from 0 to 128255
- target_logits: float32 [4096, 32], P('dp'), may hold values from -8 to 240
- vocab_map: int32 [128256], replicated, may hold values from 0 to 127999
- master: float32 [128000, 2304], P(('vocab', 'dp')), may hold values from -6 to 6
- row_moment: float32 [128000], P(('vocab', 'dp')), may hold values from 0.0001 to 0.5
- col_moment: float32 [2304], replicated, may hold values from 0.003 to 0.03
Outputs:
- direction: bfloat16 [128000, 2304], P(('vocab', 'dp'))
- row_new: float32 [128000], P(('vocab', 'dp'))
- col_new: float32 [2304], replicated
- next_rows: bfloat16 [4096, 2304], P('dp')
Inputs may be any that keep to these rules, and one draw needn't show every extreme that they name: `draft_ids`: among the 128 tokens of one index of dp, at most 20 have draft ids in any one block of 16000 consecutive ids, and some block holds exactly 20 of them.
All inputs are finite; a program needn't handle non-finite values.
Results may differ from a plain program's by a relative error of at most 0.0073.
Values may be sent and summed in bfloat16 or wider, within the bound.
No kernel may reach another device: no remote copies, remote signals or barrier semaphores. Data moves between devices by JAX's collectives and lax.ppermute only.
A program may use at most 128 MiB of HBM per device.

v0:
```python
import jax
import jax.numpy as jnp
from jax import lax
from jax.sharding import PartitionSpec as P

DECAY_RATE = 0.9
STEP_SCALE = 0.01
SQUARE_EPS = 1e-30


def body(
    draft_logits,
    hidden,
    embed_cot,
    draft_ids,
    target_ids,
    target_logits,
    vocab_map,
    master,
    row_moment,
    col_moment,
):
    tokens_here, shard_cols = draft_logits.shape
    owned_rows, features = master.shape
    dp_count = lax.axis_size("dp")
    vocab_count = lax.axis_size("vocab")
    vocab_index = lax.axis_index("vocab")
    dp_index = lax.axis_index("dp")
    logits = draft_logits.astype(jnp.float32)
    local_max = jnp.max(logits, axis=1)
    highest = lax.pmax(local_max, "vocab")
    totals = lax.psum(jnp.sum(jnp.exp(logits - highest[:, None]), axis=1), "vocab")
    probs = jnp.exp(logits - highest[:, None]) / totals[:, None]
    shifted = target_logits - jnp.max(target_logits, axis=1, keepdims=True)
    target_exp = jnp.exp(shifted)
    weights = target_exp / jnp.sum(target_exp, axis=1, keepdims=True)
    mapped = vocab_map[target_ids] - vocab_index * shard_cols
    inside = (mapped >= 0) & (mapped < shard_cols)
    token_index = jnp.broadcast_to(
        jnp.arange(tokens_here, dtype=jnp.int32)[:, None], target_ids.shape
    )
    target = (
        jnp.zeros((tokens_here, shard_cols), jnp.float32)
        .at[token_index, jnp.clip(mapped, 0, shard_cols - 1)]
        .add(jnp.where(inside, weights, jnp.zeros_like(weights)))
    )
    slopes = (probs - target).astype(jnp.bfloat16)
    owned_slopes = lax.all_to_all(slopes, "dp", split_axis=1, concat_axis=0, tiled=True)
    head_grad = jnp.einsum(
        "tv,td->vd",
        owned_slopes,
        lax.all_gather(hidden, "dp", axis=0, tiled=True),
        preferred_element_type=jnp.float32,
    )
    block_base = vocab_index * shard_cols
    in_shard = (draft_ids >= block_base) & (draft_ids < block_base + shard_cols)
    slot_count = tokens_here // vocab_count + tokens_here // (4 * vocab_count)
    position = jnp.cumsum(in_shard.astype(jnp.int32)) - 1
    placing = (position[None, :] == jnp.arange(slot_count, dtype=jnp.int32)[:, None]) & in_shard[
        None, :
    ]
    filled = jnp.any(placing, axis=1)
    packed_ids = jnp.where(filled, jnp.sum(jnp.where(placing, draft_ids[None, :], 0), axis=1), -1)
    placing_half = placing.astype(jnp.bfloat16)
    packed_cot = jnp.dot(placing_half, embed_cot, preferred_element_type=jnp.float32).astype(
        jnp.bfloat16
    )
    all_ids, all_cot = (
        lax.all_gather(packed_ids, "dp", axis=0, tiled=True),
        lax.all_gather(packed_cot, "dp", axis=0, tiled=True),
    )
    row_base = (vocab_index * dp_count + dp_index) * owned_rows
    row_iota = jnp.arange(owned_rows, dtype=jnp.int32)
    matches = (all_ids[None, :] - row_base == row_iota[:, None]).astype(jnp.bfloat16)
    grad = head_grad + jnp.dot(matches, all_cot, preferred_element_type=jnp.float32)
    squares = grad * grad + SQUARE_EPS
    row_new = DECAY_RATE * row_moment + (1.0 - DECAY_RATE) * jnp.mean(squares, axis=1)
    column_total, row_total = lax.psum(
        (jnp.sum(squares, axis=0), jnp.sum(row_new)), ("dp", "vocab")
    )
    vocab_rows = owned_rows * dp_count * vocab_count
    col_new = DECAY_RATE * col_moment + (1.0 - DECAY_RATE) * (column_total / vocab_rows)
    scale = row_new[:, None] * col_new[None, :] / (row_total / vocab_rows)
    direction = grad / jnp.sqrt(scale)
    fresh = (master - STEP_SCALE * direction).astype(jnp.bfloat16)
    wanted = all_ids - row_base
    select = (wanted[:, None] == row_iota[None, :]).astype(jnp.bfloat16)
    slot_values = lax.psum_scatter(
        jnp.dot(select, fresh, preferred_element_type=jnp.float32).astype(jnp.bfloat16),
        "dp",
        scatter_dimension=0,
        tiled=True,
    )
    spread = jnp.einsum("st,sd->td", placing_half, slot_values, preferred_element_type=jnp.float32)
    next_rows = lax.psum(spread.astype(jnp.bfloat16), "vocab")
    return (direction.astype(jnp.bfloat16), row_new, col_new, next_rows)


def solution(mesh):
    in_specs = (
        P("dp", "vocab"),
        P("dp", None),
        P("dp", None),
        P("dp"),
        P("dp", None),
        P("dp", None),
        P(),
        P(("vocab", "dp"), None),
        P(("vocab", "dp")),
        P(),
    )
    out_specs = (P(("vocab", "dp"), None), P(("vocab", "dp")), P(), P("dp", None))
    return jax.shard_map(body, mesh=mesh, in_specs=in_specs, out_specs=out_specs, check_vma=False)
```

profile of v0, /device:TPU:8, one launch (start us, length us, event | category | flops | bytes accessed | tf_op | source)
XLA Modules:
  0.0 618.9 jit_solution(5468428876925927025)
XLA Ops:
  7.2 0.7 convert_bitcast_fusion
  8.0 0.1 copy.39
  8.1 0.2 reduce-window.8
  8.3 0.1 add_reduce_fusion
  8.4 0.8 fusion.6
  9.3 0.7 all-gather.4.cloned.1.call-update
  10.0 0.7 compare_select_fusion.1
  11.0 23.0 %gather_fusion = s32[4096]{0:T(1024)S(1)} fusion(s32[128256]{0:T(1024)S(1)} %copy-done.2, s32[4096]{0:T(1024)S(1)} %broadcast_clamp_fusion), kind=kCustom, calls=%fused_computation | custom fusion | bytes 49152 | tf_op jit(solution)/shard_map/gather | solution.py:37
  34.4 0.1 copy.35
  34.8 0.2 fusion.12
  35.0 0.1 divide_select_fusion
  35.2 31.6 %scatter_custom_fusion = f32[2048000]{0:T(1024)} fusion(s32[4096]{0:T(1024)S(1)} %reshape.100, f32[4096]{0:T(1024)S(1)} %reshape.102, f32[]{:T(128)} %constant.21.clone.1), kind=kCustom, calls=%fused_computation.10 | custom fusion | flops 4096 | bytes 8192004
  66.8 9.1 %reshape.90 = f32[128,16000]{1,0:T(8,128)} reshape(f32[2048000]{0:T(1024)} %scatter_custom_fusion) | data formatting | bytes 16384000 | tf_op jit(solution)/shard_map/scatter-add | solution.py:45
  75.9 2.9 reduce_max.23
  78.8 13.1 %pmax.7 = f32[128]{0:T(128)S(1)} all-reduce(bf16[128]{0:T(256)(128)(2,1)S(1)} %reduce_max.23), channel_id=1, replica_groups=mesh['dp'=32,'vocab'=8] {'vocab'}, use_global_device_ids=true, to_apply=%region_1.0 | all-reduce | flops 128 | bytes 768 | tf_op jit(solution)/shard_map/pmax | solution.py:31
  91.9 3.7 fusion.1
  95.5 12.4 %psum.28 = f32[128]{0:T(128)S(1)} all-reduce(f32[128]{0:T(128)S(1)} %fusion.1), channel_id=1, replica_groups=mesh['dp'=32,'vocab'=8] {'vocab'}, use_global_device_ids=true, to_apply=%region_3.0 | all-reduce | flops 128 | bytes 1024 | tf_op jit(solution)/shard_map/psum | solution.py:32
  108.0 6.9 %subtract_convert_fusion = bf16[128,16000]{1,0:T(8,128)(2,1)} fusion(f32[128,16000]{1,0:T(8,128)} %reshape.90, bf16[128,16000]{1,0:T(8,128)(2,1)} %param.10, f32[128]{0:T(128)S(1)} %psum.28, f32[128]{0:T(128)S(1)} %pmax.7), kind=kLoop, calls=%fused_computation.2 | loop fusion | flops 10240000 | bytes 16385024 | tf_op jit(solution)/shard_map/convert_element_type | solution.py:47
  114.8 10.9 %reshape.126 = bf16[128,32,500]{2,1,0:T(8,128)(2,1)} reshape(bf16[128,16000]{1,0:T(8,128)(2,1)} %subtract_convert_fusion) | data formatting | bytes 8192000 | tf_op jit(solution)/shard_map/all_to_all | solution.py:48
  125.7 7.9 %copy.40 = bf16[128,32,500]{0,2,1:T(8,128)(2,1)} copy(bf16[128,32,500]{2,1,0:T(8,128)(2,1)} %reshape.126) | data formatting | bytes 8192000 | tf_op jit(solution)/shard_map/all_to_all | solution.py:48
  133.6 11.5 %all-to-all-start = ((bf16[128,32,500]{0,2,1:T(8,128)(2,1)}), bf16[128,32,500]{0,2,1:T(8,128)(2,1)}, u32[]{:S(2)}, u32[]{:S(2)}) async-start(bf16[128,32,500]{0,2,1:T(8,128)(2,1)} %copy.40), calls=%async_computation | async-start | bytes 8257536 | tf_op jit(solution)/shard_map/all_to_all | solution.py:48
  145.2 0.6 fusion.25
  146.5 0.1 fusion.16
  146.6 0.1 select_reduce_fusion
  146.7 0.1 select_dynamic-update-slice_fusion
  146.8 146.2 %all-reduce = s32[640]{0:T(1024)S(1)} all-reduce(s32[640]{0:T(1024)S(1)} %select_dynamic-update-slice_fusion), channel_id=1, replica_groups=mesh['dp'=32,'vocab'=8] {'dp'}, use_global_device_ids=true, to_apply=%add | all-reduce | flops 640 | bytes 5120
  293.0 3.8 reshape.123
  296.8 4.1 fusion.8
  301.0 6.6 %copy.38 = bf16[32,128,500]{2,1,0:T(8,128)(2,1)} copy(bf16[32,128,500]{1,2,0:T(8,128)(2,1)} %bitcast) | data formatting | bytes 8192000 | tf_op jit(solution)/shard_map/all_to_all | solution.py:48
  307.5 18.4 %all-gather.4.cloned.1.call-done = bf16[4096,2304]{1,0:T(8,128)(2,1)} async-done(((bf16[128,2304]{1,0:T(8,128)(2,1)}), bf16[4096,2304]{1,0:T(8,128)(2,1)}) %all-gather.4.cloned.1.call-update) | async-done | bytes 18874384 | tf_op jit(solution)/shard_map/all_gather | solution.py:52
  326.0 18.5 %fusion.4 = (f32[2304]{0:T(1024)S(1)}, f32[500]{0:T(512)S(1)}, f32[500,2304]{1,0:T(8,128)}) fusion(f32[500,2304]{1,0:T(8,128)} %fusion.8, bf16[4096,500]{1,0:T(8,128)(2,1)} %bitcast.14, bf16[4096,2304]{1,0:T(8,128)(2,1)} %all-gather.4.cloned.1.call-done), kind=kOutput, calls=%fused_computation.12 | convolution fusion | flops 9442941952 | bytes 32197584 | tf_op jit(solution)/shard_map/tv,td->vd/dot_general | solution.py:49
  344.5 0.6 fusion.24
  345.1 74.8 %all-reduce.3 = (f32[]{:T(128)}, f32[2304]{0:T(1024)S(1)}) all-reduce(f32[]{:T(128)} %get-tuple-element.8, f32[2304]{0:T(1024)S(1)} %get-tuple-element.4), channel_id=1, replica_groups=mesh['dp'=32,'vocab'=8] {'dp','vocab'}, use_global_device_ids=true, to_apply=%region_14.15 | all-reduce | flops 2305 | bytes 18440 | tf_op jit(solution)/shard_map/psum | solution.py:78
  420.6 5.8 convolution_convert_fusion
  426.4 79.6 %fusion = bf16[24,2304]{1,0:T(8,128)(2,1)S(1)} fusion(bf16[640,2304]{1,0:T(8,128)(2,1)S(1)} %convolution_convert_fusion), kind=kCustom, calls=%all-reduce-scatter | all-reduce-scatter fusion | flops 1769473 | bytes 3060736
  506.1 1.9 collective-permute-start.5
  508.0 2.2 collective-permute-start
  510.2 4.7 collective-permute-start.1
  514.9 3.3 collective-permute-start.2
  518.1 7.8 %collective-permute-start.3 = (bf16[24,2304]{1,0:T(8,128)(2,1)S(1)}, bf16[24,2304]{1,0:T(8,128)(2,1)S(1)}, u32[]{:S(2)}, u32[]{:S(2)}) collective-permute-start(bf16[24,2304]{1,0:T(8,128)(2,1)S(1)} %fusion), channel_id=1, source_target_pairs={{0,32},{8,40},{16,48},{24,56},{32,64},{40,72},{48,80},{56,88},{64,... | collective-permute-start | bytes 331784
  525.9 0.1 collective-permute-done.5
  526.0 8.8 %collective-permute-start.4 = (bf16[24,2304]{1,0:T(8,128)(2,1)S(1)}, bf16[24,2304]{1,0:T(8,128)(2,1)S(1)}, u32[]{:S(2)}, u32[]{:S(2)}) collective-permute-start(bf16[24,2304]{1,0:T(8,128)(2,1)S(1)} %fusion), channel_id=1, source_target_pairs={{0,40},{8,48},{16,56},{24,64},{32,72},{40,80},{48,88},{56,96},{64,... | collective-permute-start | bytes 331784
  535.5 1.6 collective-permute-done.4
  537.1 2.1 concatenate.4
  539.2 1.9 convolution_convert_fusion.1
  541.1 4.5 fusion.23
  545.6 64.8 %all-reduce.6.cloned.1.call-done = bf16[128,2304]{1,0:T(8,128)(2,1)} async-done(((bf16[128,2304]{1,0:T(8,128)(2,1)}), bf16[128,2304]{1,0:T(8,128)(2,1)}) %all-reduce.6.cloned.1.call-update) | async-done | bytes 589840 | tf_op jit(solution)/shard_map/psum | solution.py:95
  610.4 1.9 copy.43
  (62 shorter events, 1.2 us)
Async XLA Ops:
  7.2 1.2 copy-start
  7.2 3.8 copy-start.2
  7.2 285.8 %all-gather.6.cloned.1.call-start = ((), (), s32[]{:S(2)}) async-start(), calls=%async_computation.3 | async-start | bytes 3649536 | tf_op jit(solution)/shard_map/all_gather | solution.py:70
  8.0 138.6 %copy-start.9 = (pred[128]{0:T(512)(128)(4,1)}, pred[128]{0:T(512)(128)(4,1)S(1)}, u32[]{:S(2)}) copy-start(pred[128]{0:T(512)(128)(4,1)S(1)} %get-tuple-element.11) | copy-start | bytes 388
  8.4 138.2 %copy-start.8 = (s32[128]{0:T(128)}, s32[128]{0:T(128)S(1)}, u32[]{:S(2)}) copy-start(s32[128]{0:T(128)S(1)} %add_reduce_fusion) | copy-start | bytes 1540
  9.3 316.7 %all-gather.4.cloned.1.call-start = ((), (), s32[]{:S(2)}) async-start(), calls=%async_computation.1 | async-start | bytes 19464192 | tf_op jit(solution)/shard_map/all_gather | solution.py:52
  11.0 23.3 %copy-start.14 = (s32[2]{0:T(128)S(1)}, s32[2]{0:T(128)}, u32[]{:S(2)}) copy-start(s32[2]{0:T(128)} %constant.64) | copy-start | bytes 28
  11.0 23.3 %copy-start.13 = (s32[2]{0:T(128)S(1)}, s32[2]{0:T(128)}, u32[]{:S(2)}) copy-start(s32[2]{0:T(128)} %constant.67) | copy-start | bytes 28
  11.0 23.7 %copy-start.4 = (f32[128,32]{0,1:T(8,128)S(1)}, f32[128,32]{0,1:T(8,128)}, u32[]{:S(2)}) copy-start(f32[128,32]{0,1:T(8,128)} %param.15) | copy-start | bytes 49156
  133.6 11.6 %copy-start.12 = (u32[256]{0:T(256)S(1)}, u32[256]{0:T(256)}, u32[]{:S(2)}) copy-start(u32[256]{0:T(256)} %constant.74) | copy-start | bytes 3076
  133.6 13.0 %copy-start.11 = (s32[128]{0:T(128)S(1)}, s32[128]{0:T(128)}, u32[]{:S(2)}) copy-start(s32[128]{0:T(128)} %param.13) | copy-start | bytes 1540
  133.6 167.3 %all-to-all-start = ((bf16[128,32,500]{0,2,1:T(8,128)(2,1)}), bf16[128,32,500]{0,2,1:T(8,128)(2,1)}, u32[]{:S(2)}, u32[]{:S(2)}) async-start(bf16[128,32,500]{0,2,1:T(8,128)(2,1)} %copy.40), calls=%async_computation | async-start | bytes 8257536 | tf_op jit(solution)/shard_map/all_to_all | solution.py:48
  145.1 465.3 %all-reduce.6.cloned.1.call-start = ((), (), s32[]{:S(2)}) async-start(), calls=%async_computation.2 | async-start | bytes 1179648 | tf_op jit(solution)/shard_map/psum | solution.py:95
  326.0 18.5 %copy-start.10 = (f32[500]{0:T(512)S(1)}, f32[500]{0:T(512)}, u32[]{:S(2)}) copy-start(f32[500]{0:T(512)} %param.18) | copy-start | bytes 6004
  326.0 94.0 %copy-start.6 = (f32[2304]{0:T(1024)S(1)}, f32[2304]{0:T(1024)}, u32[]{:S(2)}) copy-start(f32[2304]{0:T(1024)} %param.19) | copy-start | bytes 27652
  345.1 196.0 %copy-start.7 = (f32[500]{0:T(512)}, f32[500]{0:T(512)S(1)}, u32[]{:S(2)}) copy-start(f32[500]{0:T(512)S(1)} %get-tuple-element.16) | copy-start | bytes 6004
  419.9 121.2 %copy-start.5 = (f32[2304]{0:T(1024)}, f32[2304]{0:T(1024)S(1)}, u32[]{:S(2)}) copy-start(f32[2304]{0:T(1024)S(1)} %multiply_add_fusion.1) | copy-start | bytes 27652
  506.0 29.5 %copy-start.3 = (bf16[24,2304]{1,0:T(8,128)(2,1)}, bf16[24,2304]{1,0:T(8,128)(2,1)S(1)}, u32[]{:S(2)}) copy-start(bf16[24,2304]{1,0:T(8,128)(2,1)S(1)} %fusion) | copy-start | bytes 331780
  506.1 20.0 %collective-permute-start.5 = (bf16[4,2304]{1,0:T(4,128)(2,1)S(1)}, bf16[4,2304]{1,0:T(4,128)(2,1)S(1)}, u32[]{:S(2)}, u32[]{:S(2)}) collective-permute-start(bf16[4,2304]{1,0:T(4,128)(2,1)S(1)} %slice.2), channel_id=1, source_target_pairs={{0,48},{8,56},{16,64},{24,72},{32,80},{40,88},{48,96},{56,104},{64... | collective-permute-start | bytes 55304
  508.0 27.4 %collective-permute-start = (bf16[24,2304]{1,0:T(8,128)(2,1)S(1)}, bf16[24,2304]{1,0:T(8,128)(2,1)S(1)}, u32[]{:S(2)}, u32[]{:S(2)}) collective-permute-start(bf16[24,2304]{1,0:T(8,128)(2,1)S(1)} %fusion), channel_id=1, source_target_pairs={{0,8},{8,16},{16,24},{24,32},{32,40},{40,48},{48,56},{56,64},{64,7... | collective-permute-start | bytes 331784
  510.2 25.3 %collective-permute-start.1 = (bf16[24,2304]{1,0:T(8,128)(2,1)S(1)}, bf16[24,2304]{1,0:T(8,128)(2,1)S(1)}, u32[]{:S(2)}, u32[]{:S(2)}) collective-permute-start(bf16[24,2304]{1,0:T(8,128)(2,1)S(1)} %fusion), channel_id=1, source_target_pairs={{0,16},{8,24},{16,32},{24,40},{32,48},{40,56},{48,64},{56,72},{64,... | collective-permute-start | bytes 331784
  514.9 20.6 %collective-permute-start.2 = (bf16[24,2304]{1,0:T(8,128)(2,1)S(1)}, bf16[24,2304]{1,0:T(8,128)(2,1)S(1)}, u32[]{:S(2)}, u32[]{:S(2)}) collective-permute-start(bf16[24,2304]{1,0:T(8,128)(2,1)S(1)} %fusion), channel_id=1, source_target_pairs={{0,24},{8,32},{16,40},{24,48},{32,56},{40,64},{48,72},{56,80},{64,... | collective-permute-start | bytes 331784
  518.1 17.3 %collective-permute-start.3 = (bf16[24,2304]{1,0:T(8,128)(2,1)S(1)}, bf16[24,2304]{1,0:T(8,128)(2,1)S(1)}, u32[]{:S(2)}, u32[]{:S(2)}) collective-permute-start(bf16[24,2304]{1,0:T(8,128)(2,1)S(1)} %fusion), channel_id=1, source_target_pairs={{0,32},{8,40},{16,48},{24,56},{32,64},{40,72},{48,80},{56,88},{64,... | collective-permute-start | bytes 331784
  526.0 11.1 %collective-permute-start.4 = (bf16[24,2304]{1,0:T(8,128)(2,1)S(1)}, bf16[24,2304]{1,0:T(8,128)(2,1)S(1)}, u32[]{:S(2)}, u32[]{:S(2)}) collective-permute-start(bf16[24,2304]{1,0:T(8,128)(2,1)S(1)} %fusion), channel_id=1, source_target_pairs={{0,40},{8,48},{16,56},{24,64},{32,72},{40,80},{48,88},{56,96},{64,... | collective-permute-start | bytes 331784
  537.1 75.2 %copy-start.1 = (bf16[128,2304]{1,0:T(8,128)(2,1)S(1)}, bf16[128,2304]{1,0:T(8,128)(2,1)}, u32[]{:S(2)}) copy-start(bf16[128,2304]{1,0:T(8,128)(2,1)} %param.12) | copy-start | bytes 1769476
Sparse Core Ops, SparseCore 0:
  11.2 81.9 all-gather.5
  95.8 230.1 all-gather.3
  541.2 69.1 all-reduce.5
where the time goes:
time: 620 us; the launch traced here: 619 us
  blocking collectives  326 us (53%)
  waiting for transfers between devices  85.7 us (14%)
  local copies, waits for them, and re-layouts  66.8 us (11%)
  other arithmetic  52.7 us (8%)
  starting transfers between devices  40.2 us (6%)
  matrix products  31.2 us (5%)
  between operations  16.1 us (3%)
    unnamed x2, blocking collectives  226 us
    psum x1, blocking collectives, body(): lax.psum((jnp.sum(squares, axis=0), jnp.sum(row_new)), ('dp', 'vocab'))  74.8 us
    psum x1, waiting for transfers between devices, body(): next_rows = lax.psum(spread.astype(jnp.bfloat16), 'vocab')  64.8 us
    unnamed x5, other arithmetic  31.9 us
    unnamed x6, starting transfers between devices  28.6 us
    all_to_all x3, local copies, waits for them, and re-layouts, body(): lax.all_to_all(slopes, 'dp', split_axis=1, concat_axis=0, tiled=True)  25.3 us
    gather x1, local copies, waits for them, and re-layouts, body(): mapped = vocab_map[target_ids] - vocab_index * shard_cols  23 us
    dot_general x1, matrix products, body(): jnp.einsum('tv,td->vd', owned_slopes, lax.all_gather(hidden, 'dp', axis=0...  18.5 us
  transfers between devices with their start and end apart: 10, of which 4 were waited for; matrix products, arithmetic and copies ran while one was open for 19% of the time, Pallas kernels for 0%

commit v1 on v0

v1 whole, which is shorter than its diff:
```python
import functools

import jax
import jax.numpy as jnp
from jax import lax
from jax.experimental import pallas as pl
from jax.experimental.pallas import tpu as pltpu
from jax.sharding import Mesh
from jax.sharding import PartitionSpec as P

DECAY_RATE = 0.9
STEP_SCALE = 0.01
SQUARE_EPS = 1e-30
LANES = 128
DP = ("y", "z")
VOCAB = ("x", "c")
BF16 = jnp.bfloat16
F32 = jnp.float32
VMEM_BYTES = 56 * 1024 * 1024


def stats_kernel(logits_ref, out_ref):
    tokens, cols = logits_ref.shape
    chunks = cols // LANES

    def chunk(i):
        return logits_ref[:, pl.ds(pl.multiple_of(i * LANES, LANES), LANES)].astype(F32)

    running = lax.fori_loop(
        1, chunks, lambda i, m: jnp.maximum(m, chunk(i)), chunk(0), unroll=4
    )
    top = jnp.max(running, axis=1, keepdims=True)
    total = lax.fori_loop(
        0,
        chunks,
        lambda i, s: s + jnp.exp(chunk(i) - top),
        jnp.zeros((tokens, LANES), F32),
        unroll=5,
    )
    total = jnp.sum(total, axis=1, keepdims=True)
    lane = lax.broadcasted_iota(jnp.int32, (tokens, LANES), 1)
    out_ref[...] = jnp.where(lane == 0, top, total).T[0:8, :]


def slopes_kernel(
    wanted_ref, logits_ref, stats_ref, high_ref, low_ref, weight_ref, out_ref, target, flipped, stage
):
    tokens, cols = logits_ref.shape
    dests, sent_rows, _ = out_ref.shape
    slots = wanted_ref.shape[0] // dests
    owned = cols // dests
    used = sent_rows - owned
    chunks = cols // LANES
    row = lax.broadcasted_iota(jnp.int32, (LANES, LANES), 0)

    def build(t, carry):
        high = high_ref[pl.ds(t, 1), :]
        low = low_ref[pl.ds(t, 1), :]
        weight = weight_ref[pl.ds(t, 1), :]
        left = jnp.where(high == row, weight, 0.0).astype(BF16)
        right = jnp.where(low == row, 1.0, 0.0).astype(BF16)
        target[pl.ds(pl.multiple_of(t * LANES, LANES), LANES), :] = lax.dot_general(
            left, right, (((1,), (1,)), ((), ())), preferred_element_type=F32
        )
        return carry

    lax.fori_loop(0, tokens, build, 0, unroll=4)

    stats = stats_ref[...]
    tops = stats[:, 0, :]
    sums = stats[:, 1, :]
    highest = jnp.max(tops, axis=0, keepdims=True)
    totals = jnp.sum(sums * jnp.exp(tops - highest), axis=0, keepdims=True)
    columns = jnp.where(row == 0, highest, 1.0 / totals).T
    highest_col = jnp.broadcast_to(columns[:, 0:1], (tokens, LANES))
    inverse_col = jnp.broadcast_to(columns[:, 1:2], (tokens, LANES))

    def slope(i, carry):
        start = pl.multiple_of(i * LANES, LANES)
        values = logits_ref[:, pl.ds(start, LANES)].astype(F32)
        goal = target[pl.ds(i, tokens, stride=LANES), :]
        flipped[pl.ds(start, LANES), :] = (jnp.exp(values - highest_col) * inverse_col - goal).T
        return carry

    lax.fori_loop(0, chunks, slope, 0)

    def arrange(d, carry):
        stage[0 : owned + 4, :] = flipped[pl.ds(d * owned, owned + 4), :]
        for j in range(used):
            stage[owned + j : owned + j + 1, :] = flipped[pl.ds(wanted_ref[d * slots + j], 1), :]
        out_ref[d] = stage[...].astype(BF16)
        return carry

    lax.fori_loop(0, dests, arrange, 0)


def grad_kernel(
    parity_ref,
    slopes_ref,
    own_ref,
    other_ref,
    cot_ref,
    ids_ref,
    row_ids_ref,
    moment_ref,
    grad_ref,
    row_new_ref,
    sums_ref,
):
    step = pl.program_id(0)
    per_step, rows, tokens = slopes_ref.shape
    half = own_ref.shape[2]
    features = 2 * half
    owned = rows - 20
    own_at = pl.multiple_of(parity_ref[0] * half, LANES)
    other_at = pl.multiple_of((1 - parity_ref[0]) * half, LANES)

    @pl.when(step == 0)
    def _():
        match = jnp.where(ids_ref[0:1, :] == row_ids_ref[:, 0:1], 1.0, 0.0).astype(BF16)
        slots = cot_ref.shape[1] // 2
        wide = cot_ref.shape[0] * slots
        for side in range(2):
            cot = cot_ref[:, side * slots : (side + 1) * slots, :].reshape(wide, half)
            grad_ref[:, side * half : (side + 1) * half] = jnp.dot(
                match, cot, preferred_element_type=F32
            )

    left = jnp.concatenate([slopes_ref[j] for j in range(per_step)], axis=1)
    for ref, at in ((own_ref, own_at), (other_ref, other_at)):
        right = jnp.concatenate([ref[j] for j in range(per_step)], axis=0)
        grad_ref[:, pl.ds(at, half)] += jnp.dot(left, right, preferred_element_type=F32)

    @pl.when(step == pl.num_programs(0) - 1)
    def _():
        grad = grad_ref[...]
        squares = grad * grad + SQUARE_EPS
        mean = jnp.sum(squares, axis=1, keepdims=True) * (1.0 / features)
        row_new = DECAY_RATE * moment_ref[:, 0:1] + (1.0 - DECAY_RATE) * mean
        row_new_ref[...] = jnp.broadcast_to(row_new, row_new_ref.shape)
        is_owned = lax.broadcasted_iota(jnp.int32, (rows, 1), 0) < owned
        sums_ref[:, 0:features] = jnp.sum(
            jnp.where(is_owned, squares, 0.0), axis=0, keepdims=True
        )
        row_total = jnp.sum(jnp.where(is_owned, row_new, 0.0), axis=0, keepdims=True)
        sums_ref[:, features:] = jnp.broadcast_to(row_total, (1, LANES))


def total_over_all(value, sizes):
    for axis, size in sizes:
        step = 1
        while step < size:
            value = value + lax.ppermute(value, axis, [(i, i ^ step) for i in range(size)])
            step *= 2
    return value


def body(
    sizes,
    draft_logits,
    hidden,
    embed_cot,
    draft_ids,
    target_ids,
    target_logits,
    vocab_map,
    master,
    row_moment,
    col_moment,
):
    tokens, shard_cols = draft_logits.shape
    owned, features = master.shape
    topk = target_ids.shape[1]
    dp_y, dp_z = sizes["y"], sizes["z"]
    dp_count = dp_y * dp_z
    vocab_count = sizes["x"] * sizes["c"]
    parity = lax.axis_index("c")
    vocab_index = lax.axis_index("x") * sizes["c"] + parity
    dp_index = lax.axis_index("y") * dp_z + lax.axis_index("z")
    block_base = vocab_index * shard_cols
    row_base = (vocab_index * dp_count + dp_index) * owned
    half = features // 2
    used = tokens // vocab_count + tokens // (4 * vocab_count)
    slots = 32

    block_of = jnp.sum(
        (draft_ids[:, None] >= shard_cols * jnp.arange(1, vocab_count, dtype=jnp.int32)[None, :]),
        axis=1,
        dtype=jnp.int32,
    )
    place = jnp.arange(tokens, dtype=jnp.int32)
    slot_of = jnp.sum(
        (block_of[:, None] == block_of[None, :]) & (place[None, :] < place[:, None]),
        axis=1,
        dtype=jnp.int32,
    )
    placing = (slot_of[None, :] == jnp.arange(slots, dtype=jnp.int32)[:, None]) & (
        block_of == vocab_index
    )[None, :]
    filled = jnp.any(placing, axis=1)
    packed_ids = jnp.where(filled, jnp.sum(jnp.where(placing, draft_ids[None, :], 0), axis=1), -1)
    packed_cot = jnp.dot(placing.astype(BF16), embed_cot, preferred_element_type=F32).astype(BF16)

    hidden_half = lax.dynamic_slice_in_dim(hidden, parity * half, half, 1)
    to_gather = jnp.concatenate([hidden_half, packed_cot[:, :half], packed_cot[:, half:]], axis=0)
    own = lax.all_gather(to_gather, DP, axis=0)
    other = lax.ppermute(own, "c", [(0, 1), (1, 0)])

    all_ids = lax.all_to_all(
        jnp.broadcast_to(jnp.pad(packed_ids, (0, LANES - slots))[None, None, :], (dp_count, 8, LANES)),
        DP,
        0,
        0,
        tiled=True,
    )[:, 0, :slots]

    stats = pl.pallas_call(
        stats_kernel,
        out_shape=jax.ShapeDtypeStruct((8, LANES), F32),
        compiler_params=pltpu.CompilerParams(vmem_limit_bytes=VMEM_BYTES),
    )(draft_logits)
    all_stats = lax.all_to_all(
        jnp.broadcast_to(stats[None], (vocab_count, 8, LANES)), VOCAB, 0, 0, tiled=True
    )

    target_t = target_logits.T
    target_exp = jnp.exp(target_t - jnp.max(target_t, axis=0, keepdims=True))
    weights = target_exp / jnp.sum(target_exp, axis=0, keepdims=True)
    first = lax.reduce_precision(weights, 8, 7)
    second = lax.reduce_precision(weights - first, 8, 7)
    third = lax.reduce_precision(weights - first - second, 8, 7)
    mapped = vocab_map[target_ids.T] - block_base
    spare = jnp.zeros((LANES - 3 * topk, tokens), F32)
    weight_rows = jnp.concatenate([first, second, third, spare], axis=0).T
    mapped_rows = jnp.concatenate([mapped] * 3 + [jnp.full(spare.shape, -1, jnp.int32)], axis=0).T
    high_rows = mapped_rows >> 7
    low_rows = mapped_rows & (LANES - 1)

    wanted = jnp.where(all_ids >= 0, all_ids - block_base, 0)
    sent_rows = owned + used
    vmem = pl.BlockSpec(memory_space=pltpu.VMEM)
    slopes = pl.pallas_call(
        slopes_kernel,
        in_specs=[pl.BlockSpec(memory_space=pltpu.SMEM)] + [vmem] * 5,
        out_specs=vmem,
        out_shape=jax.ShapeDtypeStruct((dp_count, sent_rows, LANES), BF16),
        scratch_shapes=[
            pltpu.VMEM((tokens * LANES, LANES), F32),
            pltpu.VMEM((shard_cols + 8, LANES), F32),
            pltpu.VMEM((sent_rows, LANES), F32),
        ],
        compiler_params=pltpu.CompilerParams(vmem_limit_bytes=VMEM_BYTES),
    )(wanted.reshape(dp_count * slots), draft_logits, all_stats, high_rows, low_rows, weight_rows)
    owned_slopes = lax.all_to_all(slopes, DP, 0, 0, tiled=True)

    moment_1 = lax.reduce_precision(row_moment, 8, 7)
    moment_2 = lax.reduce_precision(row_moment - moment_1, 8, 7)
    moment_3 = lax.reduce_precision(row_moment - moment_1 - moment_2, 8, 7)
    moments = jnp.stack([moment_1, moment_2, moment_3], axis=1)
    master_wide = jnp.concatenate(
        [master.astype(BF16), jnp.pad(moments, ((0, 0), (0, LANES - 3))).astype(BF16)], axis=1
    )
    select = (
        all_ids[:, :used].reshape(-1)[:, None] - row_base
        == jnp.arange(owned, dtype=jnp.int32)[None, :]
    ).astype(BF16)
    picked = jnp.dot(select, master_wide, preferred_element_type=F32).astype(BF16)
    wide = features + LANES
    over_y = lax.all_to_all(picked.reshape(dp_y, dp_z * used, wide), "y", 0, 0, tiled=True)
    over_y = jnp.sum(over_y.astype(F32), axis=0).astype(BF16)
    over_z = lax.all_to_all(over_y.reshape(dp_z, used, wide), "z", 0, 0, tiled=True)
    mine = jnp.sum(over_z.astype(F32), axis=0)
    wanted_master = mine[:, :features]
    wanted_moment = mine[:, features] + mine[:, features + 1] + mine[:, features + 2]

    ids_lanes = jnp.where(
        jnp.arange(slots, dtype=jnp.int32)[None, :] < used, all_ids, -2
    ).reshape(1, dp_count * slots)
    row_ids = jnp.concatenate(
        [row_base + jnp.arange(owned, dtype=jnp.int32), packed_ids[:used]]
    )[:, None]
    moment_col = jnp.concatenate([row_moment, wanted_moment])[:, None]
    per_step = 4
    steps = dp_count // per_step
    resident = lambda shape: pl.BlockSpec(shape, lambda i: (0,) * len(shape))
    grad, row_new_all, sums = pl.pallas_call(
        grad_kernel,
        grid=(steps,),
        in_specs=[
            pl.BlockSpec(memory_space=pltpu.SMEM),
            pl.BlockSpec((per_step, sent_rows, LANES), lambda i: (i, 0, 0)),
            pl.BlockSpec((per_step, tokens, half), lambda i: (i, 0, 0)),
            pl.BlockSpec((per_step, tokens, half), lambda i: (i, 0, 0)),
            pl.BlockSpec((dp_count, 2 * slots, half), lambda i: (0, tokens // (2 * slots), 0)),
            resident((1, dp_count * slots)),
            resident((sent_rows, 1)),
            resident((sent_rows, 1)),
        ],
        out_specs=[
            resident((sent_rows, features)),
            resident((sent_rows, LANES)),
            resident((1, wide)),
        ],
        out_shape=[
            jax.ShapeDtypeStruct((sent_rows, features), F32),
            jax.ShapeDtypeStruct((sent_rows, LANES), F32),
            jax.ShapeDtypeStruct((1, wide), F32),
        ],
        compiler_params=pltpu.CompilerParams(
            dimension_semantics=("arbitrary",), vmem_limit_bytes=VMEM_BYTES
        ),
    )(parity.astype(jnp.int32).reshape(1), owned_slopes, own, other, own, ids_lanes, row_ids, moment_col)

    totals = total_over_all(
        sums, (("c", sizes["c"]), ("x", sizes["x"]), ("y", dp_y), ("z", dp_z))
    )
    vocab_rows = owned * dp_count * vocab_count
    col_new = DECAY_RATE * col_moment + (1.0 - DECAY_RATE) * (totals[0, :features] / vocab_rows)
    row_mean = totals[0, features] / vocab_rows
    row_new = row_new_all[:, 0]
    by_col = lax.rsqrt(col_new)[None, :]
    by_row = lax.rsqrt(row_new / row_mean)[:, None]
    direction = (grad[:owned] * by_row[:owned] * by_col).astype(BF16)
    wanted_step = grad[owned:] * by_row[owned:] * by_col
    fresh = (wanted_master - STEP_SCALE * wanted_step).astype(BF16)
    fresh = jnp.pad(fresh, ((0, 24 - used), (0, 0)))
    all_fresh = lax.all_gather(fresh, VOCAB, axis=0, tiled=True)
    spread = (
        (block_of * 24 + slot_of)[:, None]
        == jnp.arange(24 * vocab_count, dtype=jnp.int32)[None, :]
    ).astype(BF16)
    next_rows = jnp.dot(spread, all_fresh, preferred_element_type=F32).astype(BF16)
    return direction, row_new[:owned], col_new, next_rows


def solution(mesh):
    sizes = {"y": 4, "z": 8, "x": 4, "c": 2}
    fine = Mesh(mesh.devices.reshape(4, 8, 4, 2), ("y", "z", "x", "c"))
    rows = VOCAB + DP
    in_specs = (
        P(DP, VOCAB),
        P(DP, None),
        P(DP, None),
        P(DP),
        P(DP, None),
        P(DP, None),
        P(),
        P(rows, None),
        P(rows),
        P(),
    )
    out_specs = (P(rows, None), P(rows), P(), P(DP, None))
    return jax.shard_map(
        functools.partial(body, sizes),
        mesh=fine,
        in_specs=in_specs,
        out_specs=out_specs,
        check_vma=False,
    )
```

time: 620 us -> 473 us (0.76)
  blocking collectives: 326 us -> 13.6 us
  waiting for transfers between devices: 85.7 us -> 280 us
  Pallas kernels: 0 us -> 58.1 us
  local copies, waits for them, and re-layouts: 66.8 us -> 31.8 us
  other arithmetic: 52.7 us -> 19 us
  matrix products: 31.2 us -> 5.98 us
    unnamed x2 -> x0, blocking collectives: 226 us -> none
    all_to_all x1 -> x5, waiting for transfers between devices: 0.01 us -> 129 us  [the longest x1 90.9 us: body(): owned_slopes = lax.all_to_all(slopes, DP, 0, 0, tiled=True)]
    all_gather x2 -> x1, waiting for transfers between devices: 18.4 us -> 129 us  [body(): own = lax.all_gather(to_gather, DP, axis=0)]
    psum x2 -> x0, blocking collectives: 87.2 us -> none  [the longest x1 74.8 us: body(): lax.psum((jnp.sum(squares, axis=0), jnp.sum(row_new)), ('dp', 'vocab'))]
    psum x1 -> x0, waiting for transfers between devices: 64.8 us -> none  [body(): next_rows = lax.psum(spread.astype(jnp.bfloat16), 'vocab')]
    pallas_call x0 -> x3, Pallas kernels: none -> 58.1 us  [the longest x1 29.9 us: body(): pl.pallas_call(slopes_kernel, in_specs=[pl.BlockSpec(memory_space=pltpu.S...]
    unnamed x5 -> x0, other arithmetic: 31.9 us -> none
    unnamed x6 -> x0, starting transfers between devices: 28.6 us -> none
  transfers between devices with their start and end apart: 10 -> 15, of which waited for: 4 -> 13; matrix products, arithmetic and copies ran while one was open for 19% -> 9% of each run, Pallas kernels for 0% -> 7%
where the time goes in v1:
time: 473 us; the launch traced here: 469 us
  waiting for transfers between devices  280 us (59%)
  Pallas kernels  58.1 us (12%)
  starting transfers between devices  45.1 us (10%)
  local copies, waits for them, and re-layouts  31.8 us (7%)
  other arithmetic  19 us (4%)
  between operations  15 us (3%)
  blocking collectives  13.6 us (3%)
  matrix products  5.98 us (1%)
    all_gather x1, waiting for transfers between devices, body(): own = lax.all_gather(to_gather, DP, axis=0)  129 us
    all_to_all x1, waiting for transfers between devices, body(): owned_slopes = lax.all_to_all(slopes, DP, 0, 0, tiled=True)  90.9 us
    pallas_call x1, Pallas kernels, body(): pl.pallas_call(slopes_kernel, in_specs=[pl.BlockSpec(memory_space=pltpu.S...  29.9 us
    all_to_all x1, waiting for transfers between devices, body(): lax.all_to_all(picked.reshape(dp_y, dp_z * used, wide), 'y', 0, 0, tiled=...  29.6 us
    gather x1, local copies, waits for them, and re-layouts, body(): mapped = vocab_map[target_ids.T] - block_base  23 us
    pallas_call x1, Pallas kernels, body(): pl.pallas_call(grad_kernel, grid=(steps,), in_specs=[pl.BlockSpec(memory_...  23 us
    ppermute x8, waiting for transfers between devices, total_over_all(): lax.ppermute(value, axis, [(i, i ^ step) for i in range(size)])  22.1 us
    ppermute x8, starting transfers between devices, total_over_all(): lax.ppermute(value, axis, [(i, i ^ step) for i in range(size)])  14.3 us
  transfers between devices with their start and end apart: 15, of which 13 were waited for; matrix products, arithmetic and copies ran while one was open for 9% of the time, Pallas kernels for 7%

profile of v1, /device:TPU:8, one launch (start us, length us, event | category | flops | bytes accessed | tf_op | source)
XLA Modules:
  0.0 468.6 jit_solution(12092959853731429536)
XLA Ops:
  7.3 0.8 convert_reduce_fusion.2
  8.2 1.3 convolution_convert_fusion.2
  9.6 0.8 pad_maximum_fusion
  10.4 129.3 %all-gather.3.cloned.1.call-done = bf16[6144,1152]{1,0:T(8,128)(2,1)} async-done(((bf16[192,1152]{1,0:T(8,128)(2,1)}), bf16[6144,1152]{1,0:T(8,128)(2,1)}) %all-gather.3.cloned.1.call-update) | async-done | bytes 14155792 | tf_op jit(solution)/shard_map/all_gather | solution.py:206
  139.8 0.8 select_reduce_fusion
  141.3 7.2 %all-to-all-start = ((s32[32,8,128]{2,1,0:T(8,128)}), s32[32,8,128]{2,1,0:T(8,128)S(1)}, u32[]{:S(2)}, u32[]{:S(2)}) async-start(s32[32,8,128]{2,1,0:T(8,128)} %broadcast_in_dim.49), calls=%async_computation | async-start | bytes 262144 | tf_op jit(solution)/shard_map/all_to_all | solution.py:209
  149.4 2.6 convert_element_type.40
  152.0 6.3 %all-to-all-done = s32[32,8,128]{2,1,0:T(8,128)S(1)} async-done(((s32[32,8,128]{2,1,0:T(8,128)}), s32[32,8,128]{2,1,0:T(8,128)S(1)}, u32[]{:S(2)}, u32[]{:S(2)}) %all-to-all-start) | async-done | bytes 131104 | tf_op jit(solution)/shard_map/all_to_all | solution.py:209
  158.5 3.5 convolution_convert_fusion
  162.0 6.0 %all-to-all-start.3 = ((bf16[4,160,2432]{2,1,0:T(8,128)(2,1)}), bf16[4,160,2432]{2,1,0:T(8,128)(2,1)}, u32[]{:S(2)}, u32[]{:S(2)}) async-start(bf16[4,160,2432]{2,1,0:T(8,128)(2,1)} %bitcast.36), calls=%async_computation.3 | async-start | bytes 6225920 | tf_op jit(solution)/shard_map/all_to_all | solution.py:269
  168.0 5.1 %shard_map.129 = f32[8,128]{1,0:T(8,128)} custom-call(bf16[128,16000]{1,0:T(8,128)(2,1)} %logits_ref.3), custom_call_target="tpu_custom_call" | custom-call | tf_op jit(solution)/shard_map/pallas_call | solution.py:217
  173.2 29.6 %all-to-all-done.3 = bf16[4,160,2432]{2,1,0:T(8,128)(2,1)} async-done(((bf16[4,160,2432]{2,1,0:T(8,128)(2,1)}), bf16[4,160,2432]{2,1,0:T(8,128)(2,1)}, u32[]{:S(2)}, u32[]{:S(2)}) %all-to-all-start.3) | async-done | bytes 3112992 | tf_op jit(solution)/shard_map/all_to_all | solution.py:269
  202.8 1.3 broadcast_in_dim.50
  204.1 4.3 all-to-all-start.1
  208.3 2.4 reduce_sum.61
  210.7 1.1 reshape.102
  211.8 2.0 all-to-all-done.1.stats_ref
  213.8 3.7 all-to-all-start.4
  217.7 23.0 %gather_fusion = s32[4096]{0:T(1024)S(1)} fusion(s32[128256]{0:T(1024)S(1)} %copy-done.2, s32[4096]{0:T(1024)S(1)} %fusion.15), kind=kCustom, calls=%fused_computation | custom fusion | bytes 49152 | tf_op jit(solution)/shard_map/gather | solution.py:232
  241.2 0.7 maximum_bitcast_fusion.weight_ref
  242.0 0.7 and_bitcast_fusion
  243.4 29.9 %shard_map.130 = bf16[32,520,128]{2,1,0:T(8,128)(2,1)} custom-call(s32[1024]{0:T(1024)} %select_n.36.wanted_ref, bf16[128,16000]{1,0:T(8,128)(2,1)} %logits_ref.3, f32[8,8,128]{2,1,0:T(8,128)} %copy-done.3, s32[128,128]{1,0:T(8,128)} %get-tuple-element.21.high_ref, s32[128,128]{1,0:T(8,128)} %get-tuple-element.20.low_ref, ...), custom_call_target="tpu_custom_call" | custom-call | tf_op jit(solution)/shard_map/pallas_call | solution.py:242
  273.3 9.6 %all-to-all-start.2 = ((bf16[32,520,128]{2,1,0:T(8,128)(2,1)}), bf16[32,520,128]{2,1,0:T(8,128)(2,1)}, u32[]{:S(2)}, u32[]{:S(2)}) async-start(bf16[32,520,128]{2,1,0:T(8,128)(2,1)} %shard_map.130), calls=%async_computation.2 | async-start | bytes 8519680 | tf_op jit(solution)/shard_map/all_to_all | solution.py:254
  283.1 0.8 broadcast_in_dim.90.row_ids_ref
  285.0 0.8 broadcast_in_dim.91.moment_ref
  285.9 90.9 %all-to-all-done.2.slopes_ref = bf16[32,520,128]{2,1,0:T(8,128)(2,1)} async-done(((bf16[32,520,128]{2,1,0:T(8,128)(2,1)}), bf16[32,520,128]{2,1,0:T(8,128)(2,1)}, u32[]{:S(2)}, u32[]{:S(2)}) %all-to-all-start.2) | async-done | bytes 4259872 | tf_op jit(solution)/shard_map/all_to_all | solution.py:254
  376.7 23.0 %shard_map.131 = (f32[520,2304]{1,0:T(8,128)}, f32[520,128]{1,0:T(8,128)}, f32[1,2432]{1,0:T(1,128)}) custom-call(s32[1]{0:T(128)} %bitcast.parity_ref, bf16[32,520,128]{2,1,0:T(8,128)(2,1)} %all-to-all-done.2.slopes_ref, bf16[32,192,1152]{2,1,0:T(8,128)(2,1)} %bitcast.34, bf16[32,192,1152]{2,1,0:T(8,128)(2,1)} %collective-permute-done.other_ref, ...), custom_call_target="tpu_custom_call" | custom-call | tf_op jit(solution)/shard_map/pallas_call | solution.py:286
  399.7 1.4 collective-permute-done.1
  401.1 0.7 add.93
  401.8 0.7 collective-permute-start.2
  402.6 3.2 collective-permute-done.2
  405.8 3.4 collective-permute-start.3
  409.2 1.9 collective-permute-done.3
  411.1 4.5 collective-permute-start.4
  415.5 1.6 collective-permute-done.4
  417.2 1.0 collective-permute-start.5
  418.2 4.3 collective-permute-done.5
  422.5 1.8 collective-permute-start.6
  424.2 2.0 collective-permute-done.6
  426.6 4.3 collective-permute-done.7
  430.9 2.6 collective-permute-start.8
  433.6 1.7 slice_reduce_fusion.1
  435.2 3.4 collective-permute-done.8
  439.8 1.0 divide_rsqrt_fusion
  441.7 1.1 fusion.8
  442.8 4.2 multiply_convert_fusion
  447.0 13.6 %all_gather.11 = bf16[192,2304]{1,0:T(8,128)(2,1)S(1)} all-gather(bf16[24,2304]{1,0:T(8,128)(2,1)S(1)} %pad.15), channel_id=1, replica_groups=mesh['y'=4,'z'=8,'x'=4,'c'=2] {'x','c'}, dimensions={0}, use_global_device_ids=true | all-gather | bytes 995328 | tf_op jit(solution)/shard_map/all_gather | solution.py:327
  460.6 1.2 convolution_convert_fusion.1
  (77 shorter events, 6.7 us)
Async XLA Ops:
  7.2 2.4 copy-start
  7.2 132.5 %all-gather.3.cloned.1.call-start = ((), (), s32[]{:S(2)}) async-start(), calls=%async_computation.5 | async-start | bytes 14598144 | tf_op jit(solution)/shard_map/all_gather | solution.py:206
  139.7 237.0 %collective-permute-start = (bf16[32,192,1152]{2,1,0:T(8,128)(2,1)}, bf16[32,192,1152]{2,1,0:T(8,128)(2,1)}, u32[]{:S(2)}, u32[]{:S(2)}) collective-permute-start(bf16[32,192,1152]{2,1,0:T(8,128)(2,1)} %bitcast.33), channel_id=1, source_target_pairs={{0,1},{1,0},{2,3},{3,2},{4,5},{5,4},{6,7},{7,6},{8,9},{9,8},{10,11... | collective-permute-start | bytes 42467336 | tf_op jit(solution)/shard_map/ppermute | solution.py:207
  141.3 17.0 %all-to-all-start = ((s32[32,8,128]{2,1,0:T(8,128)}), s32[32,8,128]{2,1,0:T(8,128)S(1)}, u32[]{:S(2)}, u32[]{:S(2)}) async-start(s32[32,8,128]{2,1,0:T(8,128)} %broadcast_in_dim.49), calls=%async_computation | async-start | bytes 262144 | tf_op jit(solution)/shard_map/all_to_all | solution.py:209
  162.0 40.8 %all-to-all-start.3 = ((bf16[4,160,2432]{2,1,0:T(8,128)(2,1)}), bf16[4,160,2432]{2,1,0:T(8,128)(2,1)}, u32[]{:S(2)}, u32[]{:S(2)}) async-start(bf16[4,160,2432]{2,1,0:T(8,128)(2,1)} %bitcast.36), calls=%async_computation.3 | async-start | bytes 6225920 | tf_op jit(solution)/shard_map/all_to_all | solution.py:269
  173.2 44.3 %copy-start.4 = (f32[128,32]{0,1:T(8,128)S(1)}, f32[128,32]{0,1:T(8,128)}, u32[]{:S(2)}) copy-start(f32[128,32]{0,1:T(8,128)} %param.15) | copy-start | bytes 49156
  173.2 44.6 %copy-start.5 = (s32[128,32]{0,1:T(8,128)S(1)}, s32[128,32]{0,1:T(8,128)}, u32[]{:S(2)}) copy-start(s32[128,32]{0,1:T(8,128)} %param.14) | copy-start | bytes 49156
  173.2 44.6 %copy-start.2 = (s32[128256]{0:T(1024)S(1)}, s32[128256]{0:T(1024)}, u32[]{:S(2)}) copy-start(s32[128256]{0:T(1024)} %param.16) | copy-start | bytes 1539076
  204.1 9.7 %all-to-all-start.1 = ((f32[8,8,128]{2,1,0:T(8,128)}), f32[8,8,128]{2,1,0:T(8,128)S(1)}, u32[]{:S(2)}, u32[]{:S(2)}) async-start(f32[8,8,128]{2,1,0:T(8,128)} %broadcast_in_dim.50), calls=%async_computation.1 | async-start | bytes 65536 | tf_op jit(solution)/shard_map/all_to_all | solution.py:222
  213.8 27.0 %copy-start.3 = (f32[8,8,128]{2,1,0:T(8,128)}, f32[8,8,128]{2,1,0:T(8,128)S(1)}, u32[]{:S(2)}) copy-start(f32[8,8,128]{2,1,0:T(8,128)S(1)} %all-to-all-done.1.stats_ref) | copy-start | bytes 98308
  213.8 59.5 %all-to-all-start.4 = ((bf16[8,20,2432]{2,1,0:T(8,128)(2,1)}), bf16[8,20,2432]{2,1,0:T(8,128)(2,1)S(1)}, u32[]{:S(2)}, u32[]{:S(2)}) async-start(bf16[8,20,2432]{2,1,0:T(8,128)(2,1)} %reshape.102), calls=%async_computation.4 | async-start | bytes 1867776 | tf_op jit(solution)/shard_map/all_to_all | solution.py:271
  273.3 11.7 %copy-start.7 = (f32[500]{0:T(512)S(1)}, f32[500]{0:T(512)}, u32[]{:S(2)}) copy-start(f32[500]{0:T(512)} %param.18) | copy-start | bytes 6004
  273.3 103.4 %all-to-all-start.2 = ((bf16[32,520,128]{2,1,0:T(8,128)(2,1)}), bf16[32,520,128]{2,1,0:T(8,128)(2,1)}, u32[]{:S(2)}, u32[]{:S(2)}) async-start(bf16[32,520,128]{2,1,0:T(8,128)(2,1)} %shard_map.130), calls=%async_computation.2 | async-start | bytes 8519680 | tf_op jit(solution)/shard_map/all_to_all | solution.py:254
  376.7 64.4 %copy-start.6 = (f32[2304]{0:T(1024)S(1)}, f32[2304]{0:T(1024)}, u32[]{:S(2)}) copy-start(f32[2304]{0:T(1024)} %param.19) | copy-start | bytes 27652
  399.7 1.4 collective-permute-start.1
  401.8 3.9 collective-permute-start.2
  405.8 5.3 %collective-permute-start.3 = (f32[1,2432]{1,0:T(1,128)S(1)}, f32[1,2432]{1,0:T(1,128)S(1)}, u32[]{:S(2)}, u32[]{:S(2)}) collective-permute-start(f32[1,2432]{1,0:T(1,128)S(1)} %add.94), channel_id=1, source_target_pairs={{0,4},{2,6},{4,0},{6,2},{1,5},{3,7},{5,1},{7,3},{8,12},{10,14},{12... | collective-permute-start | bytes 29192 | tf_op jit(solution)/shard_map/ppermute | solution.py:153
  411.1 6.1 %collective-permute-start.4 = (f32[1,2432]{1,0:T(1,128)S(1)}, f32[1,2432]{1,0:T(1,128)S(1)}, u32[]{:S(2)}, u32[]{:S(2)}) collective-permute-start(f32[1,2432]{1,0:T(1,128)S(1)} %add.95), channel_id=1, source_target_pairs={{0,64},{64,0},{128,192},{192,128},{1,65},{65,1},{129,193},{193,129... | collective-permute-start | bytes 29192 | tf_op jit(solution)/shard_map/ppermute | solution.py:153
  417.2 5.3 %collective-permute-start.5 = (f32[1,2432]{1,0:T(1,128)S(1)}, f32[1,2432]{1,0:T(1,128)S(1)}, u32[]{:S(2)}, u32[]{:S(2)}) collective-permute-start(f32[1,2432]{1,0:T(1,128)S(1)} %add.96), channel_id=1, source_target_pairs={{0,128},{64,192},{128,0},{192,64},{1,129},{65,193},{129,1},{193,65... | collective-permute-start | bytes 29192 | tf_op jit(solution)/shard_map/ppermute | solution.py:153
  422.5 3.8 collective-permute-start.6
  426.3 4.7 collective-permute-start.7
  430.9 7.7 %collective-permute-start.8 = (f32[1,2432]{1,0:T(1,128)S(1)}, f32[1,2432]{1,0:T(1,128)S(1)}, u32[]{:S(2)}, u32[]{:S(2)}) collective-permute-start(f32[1,2432]{1,0:T(1,128)S(1)} %add.99), channel_id=1, source_target_pairs={{0,32},{8,40},{16,48},{24,56},{32,0},{40,8},{48,16},{56,24},{1,33}... | collective-permute-start | bytes 29192 | tf_op jit(solution)/shard_map/ppermute | solution.py:153
  441.7 20.1 %copy-start.1 = (bf16[128,2304]{1,0:T(8,128)(2,1)S(1)}, bf16[128,2304]{1,0:T(8,128)(2,1)}, u32[]{:S(2)}) copy-start(bf16[128,2304]{1,0:T(8,128)(2,1)} %param.11) | copy-start | bytes 1769476
Sparse Core Ops, SparseCore 0:
  11.1 128.5 all-gather.2
